TPU v7x, 256 devices: a whole 4x4x8 slice. The times are simulated.
256 devices in a mesh: ctx: 32 (over y, z), head: 8 (over x, core).
Axes of the slice: x: 4, y: 4, z: 8, core: 2. Of those that a mesh axis runs over, the one named last changes fastest.
Arguments:
- queries: bfloat16 [16384, 8192], P('ctx', 'head'), may hold values from -6 to 6
- keys: bfloat16 [16384, 8192], P('ctx', 'head'), may hold values from -6 to 6
- values: bfloat16 [16384, 8192], P('ctx', 'head'), may hold values from -36 to 36
- out_grad: bfloat16 [16384, 8192], P('ctx', 'head'), may hold values from -6 to 6
- gain: float32 [8192], P('head'), may hold values from 0.25 to 1.75
- decay_rate: int32 [64], P('head'), may hold values from 9 to 42
- doc_lengths: int32 [8], replicated, may hold values from 1 to 10240, 16384 in all
Outputs:
- normed: bfloat16 [16384, 8192], P('ctx', 'head')
- query_grad: bfloat16 [16384, 8192], P('ctx', 'head')
- key_grad: bfloat16 [16384, 8192], P('ctx', 'head')
- value_grad: bfloat16 [16384, 8192], P('ctx', 'head')
Inputs may be any that keep to these rules, and one draw needn't show every extreme that they name: `doc_lengths`: the documents fill the 16384 positions in order; the longest has exactly 10240 positions.
All inputs are finite; a program needn't handle non-finite values.
Results may differ from a plain program's by a relative error of at most 0.0056.
Values sent between devices are 32-bit elements; how exact they have to be, the bound alone decides.
A program may use at most 128 MiB of HBM per device.

v0:
```python
import jax
import jax.numpy as jnp
from jax import lax
from jax.sharding import PartitionSpec as P

HEADS = 64
HD = 128


FULL_PRECISION = lax.Precision.HIGHEST
EPSILON = 1e-05


def prefix(value, axis, combine, identity, reverse):
    size, place = (lax.axis_size(axis), lax.axis_index(axis))
    everything = jax.tree.map(lambda part: lax.all_gather(part, axis), value)
    start = jax.tree.map(
        lambda part, zero: jnp.broadcast_to(jnp.asarray(zero, part.dtype), part.shape),
        value,
        identity,
    )

    def lap(k, before):
        at = size - 1 - k if reverse else k
        reached = at > place if reverse else at < place
        new = combine(before, jax.tree.map(lambda part: part[at], everything))
        return jax.tree.map(lambda a, b: jnp.where(reached, a, b), new, before)

    return lax.fori_loop(0, size, lap, start)


def document_ids(positions, lengths):
    ends = jnp.cumsum(lengths)
    return jnp.sum((positions[:, None] >= ends[None, :]).astype(jnp.int32), axis=1)


def block_flags(starts, block_rows, lengths):
    last_doc = document_ids(starts + block_rows - 1, lengths)
    before_doc = document_ids(jnp.maximum(starts - 1, 0), lengths)
    before_doc = jnp.where(starts > 0, before_doc, -1)
    return (last_doc, before_doc)


def decay_tables(start, block_rows, lengths, log_decay):
    positions = start + jnp.arange(block_rows, dtype=jnp.int32)
    row_docs = document_ids(positions, lengths)
    last_doc, before_doc = block_flags(start[None], block_rows, lengths)
    alive = row_docs == before_doc[0]
    reach = row_docs == last_doc[0]
    offsets = jnp.arange(block_rows).astype(jnp.float32)
    spacing = offsets[:, None] - offsets[None, :]
    causal = (spacing >= 0) & (row_docs[:, None] == row_docs[None, :])
    inner_decay = jnp.where(
        causal[None], jnp.exp(jnp.maximum(spacing, 0.0)[None] * log_decay[:, None, None]), 0.0
    )
    entry_decay = jnp.where(alive[None], jnp.exp((offsets + 1.0)[None] * log_decay[:, None]), 0.0)
    exit_decay = jnp.where(
        reach[None], jnp.exp((block_rows - 1.0 - offsets)[None] * log_decay[:, None]), 0.0
    )
    carry_decay = jnp.exp(block_rows * log_decay) * alive[block_rows - 1].astype(jnp.float32)
    return (inner_decay, entry_decay, exit_decay, carry_decay)


def combine_pair(earlier, later):
    return (earlier[0] * later[0], later[0][:, None, None] * earlier[1] + later[1])


def per_device(queries, keys, values, out_grad, gain, decay_rate, doc_lengths):
    block_rows = queries.shape[0]
    heads_here = decay_rate.shape[0]
    head_width = queries.shape[1] // heads_here
    layout = (block_rows, heads_here, head_width)
    query_rows = queries.reshape(layout)
    key_rows = keys.reshape(layout)
    value_rows = values.reshape(layout)
    grad_rows = out_grad.reshape(layout)
    gain_heads = gain.reshape(heads_here, head_width)
    features = HEADS * HD
    shard_index = lax.axis_index("ctx")
    log_decay = -jnp.exp2(-decay_rate.astype(jnp.float32) / 2.0)
    start = shard_index * block_rows
    inner_decay, entry_decay, exit_decay, carry_decay = decay_tables(
        start, block_rows, doc_lengths, log_decay
    )
    entry_t = entry_decay.T[:, :, None]
    exit_t = exit_decay.T[:, :, None]
    scores = jnp.einsum("thd,shd->hts", query_rows, key_rows, preferred_element_type=jnp.float32)
    weights = (scores * inner_decay).astype(jnp.bfloat16)
    key_scaled = (key_rows.astype(jnp.float32) * exit_t).astype(jnp.bfloat16)
    local_state = jnp.einsum(
        "thd,the->hde", key_scaled, value_rows, preferred_element_type=jnp.float32
    )
    inner_out = jnp.einsum("hts,she->the", weights, value_rows, preferred_element_type=jnp.float32)
    identity = (jnp.ones_like(carry_decay), jnp.zeros_like(local_state))
    _, state_before = prefix((carry_decay, local_state), "ctx", combine_pair, identity, False)
    query_wide = query_rows.astype(jnp.float32)
    attended = inner_out + entry_t * jnp.einsum(
        "thd,hde->the", query_wide, state_before, precision=FULL_PRECISION
    )
    grad_gain = grad_rows.astype(jnp.float32) * gain_heads[None]
    square_part = jnp.sum(attended * attended, axis=(1, 2))
    dot_part = jnp.sum(grad_gain * attended, axis=(1, 2))
    square_sum, dot_sum = lax.psum((square_part, dot_part), "head")
    inv_rms = lax.rsqrt(square_sum / features + EPSILON)[:, None, None]
    normed = (attended * inv_rms * gain_heads[None]).astype(jnp.bfloat16)
    grad_out = (
        inv_rms * (grad_gain - attended * (inv_rms * inv_rms) * dot_sum[:, None, None] / features)
    ).astype(jnp.bfloat16)
    query_scaled = (query_wide * entry_t).astype(jnp.bfloat16)
    local_grad = jnp.einsum(
        "thd,the->hde", query_scaled, grad_out, preferred_element_type=jnp.float32
    )
    grad_scores = jnp.einsum(
        "the,she->hts", grad_out, value_rows, preferred_element_type=jnp.float32
    )
    grad_weights = (grad_scores * inner_decay).astype(jnp.bfloat16)
    state_term = jnp.einsum(
        "the,hde->thd", grad_out.astype(jnp.float32), state_before, precision=FULL_PRECISION
    )
    query_grad = (
        jnp.einsum("hts,shd->thd", grad_weights, key_rows, preferred_element_type=jnp.float32)
        + entry_t * state_term
    ).astype(jnp.bfloat16)
    key_part = jnp.einsum(
        "hts,thd->shd", grad_weights, query_rows, preferred_element_type=jnp.float32
    )
    value_part = jnp.einsum("hts,the->she", weights, grad_out, preferred_element_type=jnp.float32)
    _, grad_after = prefix((carry_decay, local_grad), "ctx", combine_pair, identity, True)
    value_wide = value_rows.astype(jnp.float32)
    key_wide = key_rows.astype(jnp.float32)
    key_grad = (
        key_part
        + exit_t * jnp.einsum("she,hde->shd", value_wide, grad_after, precision=FULL_PRECISION)
    ).astype(jnp.bfloat16)
    value_grad = (
        value_part
        + exit_t * jnp.einsum("shd,hde->she", key_wide, grad_after, precision=FULL_PRECISION)
    ).astype(jnp.bfloat16)
    flat = (block_rows, heads_here * head_width)
    return (
        normed.reshape(flat),
        query_grad.reshape(flat),
        key_grad.reshape(flat),
        value_grad.reshape(flat),
    )


def solution(mesh):
    in_specs = (
        P("ctx", "head"),
        P("ctx", "head"),
        P("ctx", "head"),
        P("ctx", "head"),
        P("head"),
        P("head"),
        P(),
    )
    out_specs = (P("ctx", "head"), P("ctx", "head"), P("ctx", "head"), P("ctx", "head"))
    return jax.shard_map(
        per_device, mesh=mesh, in_specs=in_specs, out_specs=out_specs, check_vma=False
    )
```

profile of v0, /device:TPU:1, one launch (start us, length us, event | category | flops | bytes accessed | tf_op | source)
XLA Modules:
  0.0 415.7 jit_solution(14501858966864696617)
XLA Ops:
  11.5 1.5 copy.72
  14.6 1.3 fusion.9
  15.9 64.9 %all-reduce = f32[256]{0:T(256)S(1)} all-reduce(f32[256]{0:T(256)S(1)} %get-tuple-element.318), channel_id=2, replica_groups=mesh['ctx'=32,'head'=8] {'ctx'}, use_global_device_ids=true, to_apply=%add | all-reduce | flops 256 | bytes 2048
  80.9 1.5 copy.71
  82.4 2.6 copy.79
  85.5 4.2 %multiply_convert_fusion.1 = bf16[8,512,512]{2,1,0:T(8,128)(2,1)S(1)} fusion(f32[8]{0:T(128)S(1)} %get-tuple-element.319, f32[512,512]{1,0:T(8,128)S(1)} %subtract_maximum_fusion, pred[512,512]{1,0:T(8,128)(4,1)S(1)} %fusion.18, bf16[512,8,128]{0,2,1:T(8,128)(2,1)S(1)} %bitcast.106, bf16[512,8,128]{0,2,1:T(8,128)(2,1)} %bitcast.111), kind=kOutput, calls=%fused_computation.7 | convolution fusion | flops 545259520 | bytes 7602208 | tf_op jit(solution)/shard_map/thd,shd->hts/dot_general | solution.py:87
  89.7 1.9 copy-done.1
  91.6 2.9 fusion.11
  94.5 65.4 %all-gather.6.cloned.1.call-done = f32[256,128,128]{2,1,0:T(8,128)} async-done(((f32[8,128,128]{2,1,0:T(8,128)}), f32[256,128,128]{2,1,0:T(8,128)}) %all-gather.6.cloned.1.call-update) | async-done | bytes 16777232 | tf_op jit(solution)/shard_map/all_gather | solution.py:16
  159.9 39.0 %while.30 = (s32[]{:T(128)}, f32[8,128,128]{2,1,0:T(8,128)S(1)}, s32[]{:T(128)}, f32[32,8]{1,0:T(8,128)S(1)}, f32[32,8,128,128]{3,2,1,0:T(8,128)}, /*index=5*/s32[]{:T(128)}, s32[]{:T(128)}) while((s32[]{:T(128)}, f32[8,128,128]{2,1,0:T(8,128)S(1)}, s32[]{:T(128)}, f32[32,8]{1,0:T(8,128)S(1)}, f32[32,8,128,128]{3,2,1,0:T(8,128)}, ...), condition=%wide.region_5.6_spmd.clone, body=%wide.region_4.5_spmd.clone.sunk | while | flops 524292 | bytes 1573073 | solution.py:29
  161.2 1.2 fusion.55
  162.4 1.2 fusion.55
  163.6 1.2 fusion.55
  164.8 1.2 fusion.55
  166.0 1.2 fusion.55
  167.3 1.2 fusion.55
  168.5 1.2 fusion.55
  169.7 1.2 fusion.55
  170.9 1.2 fusion.55
  172.1 1.2 fusion.55
  173.4 1.2 fusion.55
  174.6 1.2 fusion.55
  175.8 1.2 fusion.55
  177.0 1.2 fusion.55
  178.2 1.2 fusion.55
  179.4 1.2 fusion.55
  180.7 1.2 fusion.55
  181.9 1.2 fusion.55
  183.1 1.2 fusion.55
  184.3 1.2 fusion.55
  185.5 1.2 fusion.55
  186.8 1.2 fusion.55
  188.0 1.2 fusion.55
  189.2 1.2 fusion.55
  190.4 1.2 fusion.55
  191.6 1.2 fusion.55
  192.8 1.2 fusion.55
  194.1 1.2 fusion.55
  195.3 1.2 fusion.55
  196.5 1.2 fusion.55
  197.7 1.2 fusion.55
  198.9 5.0 %multiply_reduce_fusion = (f32[512]{0:T(512)S(1)}, f32[512]{0:T(512)S(1)}, f32[512,8,128]{0,2,1:T(8,128)}) fusion(f32[512,1024]{0,1:T(8,128)} %copy.79, f32[8,128]{1,0:T(8,128)S(1)} %bitcast.120, f32[8,128,128]{2,1,0:T(8,128)S(1)} %get-tuple-element.230, bf16[512,8,128]{0,2,1:T(8,128)(2,1)S(1)} %bitcast.107, f32[512,8]{0,1:T(8,128)S(1)} %get-tuple-element.316, ...), kind=kOutput, calls=%fused_computation.22 | convolution fusion | flops 808975360 | bytes 7888896 | tf_op jit(solution)/shard_map/thd,hde->the/dot_general | solution.py:97
  203.9 13.0 %all-reduce.1 = (f32[512]{0:T(512)S(1)}, f32[512]{0:T(512)S(1)}) all-reduce(f32[512]{0:T(512)S(1)} %get-tuple-element.285, f32[512]{0:T(512)S(1)} %get-tuple-element.284), channel_id=1, replica_groups=mesh['ctx'=32,'head'=8] {'head'}, use_global_device_ids=true, to_apply=%region_7.8 | all-reduce | flops 1024 | bytes 8192 | tf_op jit(solution)/shard_map/psum | solution.py:103
  216.9 3.9 multiply_convert_fusion.3
  221.7 1.2 fusion.10
  223.0 2.3 copy.87
  225.3 4.2 %multiply_convert_fusion = bf16[8,512,512]{2,1,0:T(8,128)(2,1)S(1)} fusion(f32[8]{0:T(128)S(1)} %get-tuple-element.319, f32[512,512]{1,0:T(8,128)} %copy-done.9, pred[512,512]{1,0:T(8,128)(4,1)S(1)} %fusion.18, bf16[512,8,128]{0,2,1:T(8,128)(2,1)} %copy-done.4, bf16[512,1024]{1,0:T(8,128)(2,1)S(1)} %copy-done), kind=kOutput, calls=%fused_computation.6 | convolution fusion | flops 545259520 | bytes 7602208 | tf_op jit(solution)/shard_map/the,she->hts/dot_general | solution.py:113
  229.5 1.5 fusion.28
  231.5 2.2 fusion.7
  233.7 2.3 copy.88
  235.9 4.7 %fusion.29 = f32[8,128,512]{2,1,0:T(8,128)} fusion(bf16[512,8,128]{0,2,1:T(8,128)(2,1)} %copy-done.4, bf16[8,512,512]{2,1,0:T(8,128)(2,1)} %copy-done.1), kind=kOutput, calls=%fused_computation.60 | convolution fusion | flops 536870912 | bytes 7340032 | tf_op jit(solution)/shard_map/hts,the->she/dot_general | solution.py:127
  240.7 2.1 fusion.30
  242.8 116.9 %all-gather.8.cloned.1.call-done = f32[256,128,128]{2,1,0:T(8,128)} async-done(((f32[8,128,128]{2,1,0:T(8,128)}), f32[256,128,128]{2,1,0:T(8,128)}) %all-gather.8.cloned.1.call-update) | async-done | bytes 16777232 | tf_op jit(solution)/shard_map/all_gather | solution.py:16
  359.7 39.2 %while.31 = (s32[]{:T(128)}, f32[8,128,128]{2,1,0:T(8,128)S(1)}, s32[]{:T(128)}, f32[32,8]{1,0:T(8,128)S(1)}, f32[32,8,128,128]{3,2,1,0:T(8,128)}, /*index=5*/s32[]{:T(128)}, s32[]{:T(128)}, s32[]{:T(128)}, s32[]{:T(128)}) while((s32[]{:T(128)}, f32[8,128,128]{2,1,0:T(8,128)S(1)}, s32[]{:T(128)}, f32[32,8]{1,0:T(8,128)S(1)}, ...), condition=%wide.region_11.12_spmd.clone, body=%wide.region_10.11_spmd.clone.sunk | while | flops 524296 | bytes 1573135 | solution.py:29
  359.7 1.3 fusion.56
  363.5 1.2 fusion.56
  364.7 1.2 fusion.56
  369.6 1.2 fusion.56
  370.8 1.2 fusion.56
  374.5 1.2 fusion.56
  398.9 3.7 fusion.3
  402.6 2.3 copy.90
  404.9 2.6 fusion.5
  407.5 1.3 copy.89
  (138 shorter events, 38.3 us)
Async XLA Ops:
  7.2 7.4 %copy-start = (bf16[512,1024]{1,0:T(8,128)(2,1)S(1)}, bf16[512,1024]{1,0:T(8,128)(2,1)}, u32[]{:S(2)}) copy-start(bf16[512,1024]{1,0:T(8,128)(2,1)} %param.13) | copy-start | bytes 3145732
  7.2 5.8 %copy-start.12 = (u32[256]{0:T(256)S(1)}, u32[256]{0:T(256)}, u32[]{:S(2)}) copy-start(u32[256]{0:T(256)} %constant.118) | copy-start | bytes 3076
  7.2 7.1 %copy-start.11 = (s32[8]{0:T(128)S(1)}, s32[8]{0:T(128)}, u32[]{:S(2)}) copy-start(s32[8]{0:T(128)} %param.16) | copy-start | bytes 100
  7.2 152.7 %all-gather.6.cloned.1.call-start = ((), (), s32[]{:S(2)}) async-start(), calls=%async_computation | async-start | bytes 17301504 | tf_op jit(solution)/shard_map/all_gather | solution.py:16
  13.0 67.8 %copy-start.6 = (bf16[512,1024]{0,1:T(8,128)(2,1)}, bf16[512,1024]{0,1:T(8,128)(2,1)S(1)}, u32[]{:S(2)}) copy-start(bf16[512,1024]{0,1:T(8,128)(2,1)S(1)} %copy.72) | copy-start | bytes 3145732
  15.8 343.9 %all-gather.8.cloned.1.call-start = ((), (), s32[]{:S(2)}) async-start(), calls=%async_computation.1 | async-start | bytes 17301504 | tf_op jit(solution)/shard_map/all_gather | solution.py:16
  85.5 4.2 %copy-start.9 = (f32[512,512]{1,0:T(8,128)}, f32[512,512]{1,0:T(8,128)S(1)}, u32[]{:S(2)}) copy-start(f32[512,512]{1,0:T(8,128)S(1)} %subtract_maximum_fusion) | copy-start | bytes 3145732
  89.7 1.9 copy-start.1
  159.9 39.0 %copy-start.10 = (f32[1024]{0:T(1024)S(1)}, f32[1024]{0:T(1024)}, u32[]{:S(2)}) copy-start(f32[1024]{0:T(1024)} %param.15) | copy-start | bytes 12292
  220.8 1.0 copy-start.4
  225.3 4.2 %copy-start.7 = (bf16[512,1024]{0,1:T(8,128)(2,1)S(1)}, bf16[512,1024]{0,1:T(8,128)(2,1)}, u32[]{:S(2)}) copy-start(bf16[512,1024]{0,1:T(8,128)(2,1)} %copy-done.6) | copy-start | bytes 3145732
  229.5 2.0 copy-start.2
  229.5 2.0 copy-start.5
  235.9 4.8 %copy-start.3 = (bf16[8,512,512]{2,1,0:T(8,128)(2,1)S(1)}, bf16[8,512,512]{2,1,0:T(8,128)(2,1)}, u32[]{:S(2)}) copy-start(bf16[8,512,512]{2,1,0:T(8,128)(2,1)} %copy-done.2) | copy-start | bytes 12582916
  359.7 39.2 %copy-start.8 = (bf16[512,1024]{0,1:T(8,128)(2,1)S(1)}, bf16[512,1024]{0,1:T(8,128)(2,1)}, u32[]{:S(2)}) copy-start(bf16[512,1024]{0,1:T(8,128)(2,1)} %copy-done.6) | copy-start | bytes 3145732
Sparse Core Ops, SparseCore 0:
  16.0 143.9 all-gather.5
  223.1 136.5 all-gather.7
where the time goes:
time: 419 us; the launch traced here: 416 us
  waiting for transfers between devices  182 us (43%)
  other arithmetic  82.1 us (20%)
  blocking collectives  77.9 us (19%)
  matrix products  35.6 us (8%)
  local copies, waits for them, and re-layouts  19.2 us (5%)
  between operations  16.3 us (4%)
    all_gather x2, waiting for transfers between devices, prefix(): everything = jax.tree.map(lambda part: lax.all_gather(part, axis), value)  182 us
    select_n x64, other arithmetic, lap(): return jax.tree.map(lambda a, b: jnp.where(reached, a, b), new, before)  75.3 us
    unnamed x1, blocking collectives  64.9 us
    unnamed x34, local copies, waits for them, and re-layouts  15.3 us
    psum x1, blocking collectives, per_device(): square_sum, dot_sum = lax.psum((square_part, dot_part), 'head')  13 us
  transfers between devices with their start and end apart: 2, of which 2 were waited for; matrix products, arithmetic and copies ran while one was open for 7% of the time, Pallas kernels for 0%

commit v1 on v0

v1 whole, which is shorter than its diff:
```python
import jax
import jax.numpy as jnp
from jax import lax
from jax.experimental import pallas as pl
from jax.experimental.pallas import tpu as pltpu
from jax.sharding import PartitionSpec as P

EPSILON = 1e-05
FAR = 1e30
TILE = 256
MESH = pl.DeviceIdType.MESH
F32, BF16 = jnp.float32, jnp.bfloat16


def matmul(a, b):
    return lax.dot_general(a, b, (((1,), (0,)), ((), ())), preferred_element_type=F32)


def matmul_t(a, b):
    return lax.dot_general(a, b, (((1,), (1,)), ((), ())), preferred_element_type=F32)


def halves(x):
    high = x.astype(BF16)
    low = (x - high.astype(F32)).astype(BF16)
    return high, low


def twice(x):
    return jnp.concatenate([x, x], axis=1)


def make_kernel(n_ctx, n_head, n_y, n_z, rows, heads, hd, features):
    rows_own = heads * hd // n_ctx
    owners = hd // rows_own
    away = [(dy, dz) for dy in range(n_y) for dz in range(n_z) if (dy, dz) != (0, 0)]
    away.sort(key=lambda d: -(min(d[0], n_y - d[0]) + 1.01 * min(d[1], n_z - d[1])))

    def kernel(
        lengths, rates, gain, q_hbm, k_hbm, v_hbm, g_hbm,
        normed_hbm, qg_hbm, kg_hbm, vg_hbm,
        q, k, v, g, normed, qg, kg, vg,
        local1, inbox1, outbox1, state1, local2, inbox2, outbox2, state2,
        weights, attended, grad_out, spacing, entry_far, exit_far,
        square_acc, dot_acc, part, parts, key_part, value_part, carry_table,
        in_sem, out_sem, send1, recv1, send2, recv2, send3, recv3, send4, recv4, send_p, recv_p,
    ):
        me = lax.axis_index("ctx")
        me_h = lax.axis_index("head")
        y, z = me // n_z, me % n_z
        peers = [((y + dy) % n_y) * n_z + (z + dz) % n_z for dy, dz in away]

        loads = [
            pltpu.make_async_copy(src, dst, in_sem.at[i])
            for i, (src, dst) in enumerate(((k_hbm, k), (v_hbm, v), (q_hbm, q), (g_hbm, g)))
        ]
        for load in loads:
            load.start()
        barrier = pltpu.get_barrier_semaphore()
        for peer in peers:
            pl.semaphore_signal(barrier, inc=1, device_id={"ctx": peer}, device_id_type=MESH)
        for step in range(1, n_head):
            pl.semaphore_signal(
                barrier, inc=1, device_id={"head": (me_h + step) % n_head}, device_id_type=MESH
            )

        ends = []
        total = jnp.int32(0)
        for j in range(lengths.shape[0]):
            total = total + lengths[j]
            ends.append(total)

        def doc_of(position):
            count = (position >= ends[0]).astype(jnp.int32)
            for end in ends[1:]:
                count = count + (position >= end).astype(jnp.int32)
            return count

        start = me * rows
        last_doc = doc_of(start + rows - 1)
        before_doc = jnp.where(start > 0, doc_of(start - 1), -1)
        offset = lax.broadcasted_iota(jnp.int32, (rows, hd), 0)
        doc_col = doc_of(start + offset)
        offset_f = offset.astype(F32)
        entry_far[...] = jnp.where(doc_col == before_doc, offset_f + 1.0, FAR)
        exit_far[...] = jnp.where(doc_col == last_doc, rows - 1.0 - offset_f, FAR)

        def decay_row(h):
            rate = rates[h].astype(F32)
            return -jnp.exp2(jnp.full((1, hd), 1.0, F32) * (rate * -0.5))

        def cols(h):
            return pl.ds(pl.multiple_of(h * hd, hd), hd)

        own_head = me // owners
        block = lax.broadcasted_iota(jnp.int32, (n_ctx, hd), 0)
        inside = jnp.zeros((n_ctx, hd), jnp.int32)
        for end in ends:
            hit = (end >= block * rows) & (end < block * rows + rows)
            inside = inside + hit.astype(jnp.int32)
        whole = (inside == 0) & (block > 0)
        carry_table[...] = jnp.where(whole, jnp.exp(decay_row(own_head) * float(rows)), 0.0)

        loads[0].wait()
        loads[1].wait()

        @pl.loop(0, heads)
        def _(h):
            fade = jnp.exp(exit_far[...] * decay_row(h))
            scaled = (k[:, cols(h)].astype(F32) * fade).astype(BF16)
            state = matmul(scaled.T, v[:, cols(h)])
            local1[pl.ds(h * owners, owners)] = state.reshape(owners, rows_own, hd)

        pl.semaphore_wait(barrier, n_ctx - 1 + n_head - 1)

        def spread(src, dst, send, recv):
            for peer in peers:
                pltpu.make_async_remote_copy(
                    src_ref=src.at[peer], dst_ref=dst.at[me], send_sem=send.at[peer],
                    recv_sem=recv.at[me], device_id={"ctx": peer}, device_id_type=MESH,
                ).start()

        def arrived(dst, recv, send, slot):
            pltpu.make_async_remote_copy(
                src_ref=dst.at[slot], dst_ref=dst.at[slot], send_sem=send.at[slot],
                recv_sem=recv.at[slot], device_id={"ctx": slot}, device_id_type=MESH,
            ).wait_recv()

        def arrived_all(dst, recv, send):
            for peer in peers:
                arrived(dst, recv, send, peer)

        def left_all(src, dst, send, recv):
            for peer in peers:
                pltpu.make_async_remote_copy(
                    src_ref=src.at[peer], dst_ref=dst.at[me], send_sem=send.at[peer],
                    recv_sem=recv.at[me], device_id={"ctx": peer}, device_id_type=MESH,
                ).wait_send()

        spread(local1, inbox1, send1, recv1)
        inbox1[pl.ds(me, 1)] = local1[pl.ds(me, 1)]

        row_pos = start + lax.broadcasted_iota(jnp.int32, (8, rows), 1)
        doc_row = doc_of(row_pos)[0:1]
        for c in range(rows // hd):
            piece = slice(c * hd, (c + 1) * hd)
            gap = offset - (lax.broadcasted_iota(jnp.int32, (rows, hd), 1) + c * hd)
            same = (doc_col == doc_row[:, piece]) & (gap >= 0)
            spacing[:, piece] = jnp.where(same, gap.astype(F32), FAR)
        loads[2].wait()
        loads[3].wait()

        tiles = [(i * TILE, (i + 1) * TILE) for i in range(rows // TILE)]

        def wide(row, n):
            return jnp.concatenate([row] * (n // hd), axis=1)

        def forward(h):
            rate = decay_row(h)
            key_h, value_h = k[:, cols(h)], v[:, cols(h)]
            for lo, hi in tiles:
                scores = matmul_t(q[lo:hi, cols(h)], key_h[:hi])
                inner = jnp.exp(spacing[lo:hi, :hi] * wide(rate, hi))
                w = (scores * inner).astype(BF16)
                weights[h, lo:hi, :hi] = w
                attended[lo:hi, cols(h)] = matmul(w, value_h[:hi])

        half = heads // 2

        @pl.loop(0, half)
        def _(h):
            forward(h)

        arrived_all(inbox1, recv1, send1)

        def prefix(inbox, outbox, state, reverse):
            def lap(i, carried):
                j = n_ctx - 1 - i if reverse else i
                outbox[pl.ds(j, 1)] = carried[None]
                return carried * carry_table[pl.ds(j, 1), :] + inbox[j]

            lax.fori_loop(0, n_ctx, lap, jnp.zeros((rows_own, hd), F32))
            state[pl.ds(me, 1)] = outbox[pl.ds(me, 1)]

        prefix(inbox1, outbox1, state1, False)
        spread(outbox1, state1, send2, recv2)

        @pl.loop(half, heads)
        def _(h):
            forward(h)

        arrived_all(state1, recv2, send2)
        square_acc[...] = jnp.zeros_like(square_acc)
        dot_acc[...] = jnp.zeros_like(dot_acc)

        @pl.loop(0, heads)
        def _(h):
            high, low = halves(state1[pl.ds(h * owners, owners)].reshape(hd, hd))
            far = matmul(twice(q[:, cols(h)]), jnp.concatenate([high, low], axis=0))
            fade = jnp.exp(entry_far[...] * decay_row(h))
            att = attended[:, cols(h)] + fade * far
            attended[:, cols(h)] = att
            square_acc[...] += att * att
            dot_acc[...] += (g[:, cols(h)].astype(F32) * gain[pl.ds(h, 1), :]) * att

        def row_sums(x):
            return jnp.broadcast_to(jnp.sum(x, axis=1, keepdims=True), x.shape).T[0:8]

        first = lax.broadcasted_iota(jnp.int32, (8, rows), 0) < 4
        part[...] = jnp.where(first, row_sums(square_acc[...]), row_sums(dot_acc[...]))

        def part_copy(step):
            peer = (me_h + step) % n_head
            return pltpu.make_async_remote_copy(
                src_ref=part, dst_ref=parts.at[me_h], send_sem=send_p.at[peer],
                recv_sem=recv_p.at[me_h], device_id={"head": peer}, device_id_type=MESH,
            )

        for step in range(1, n_head):
            part_copy(step).start()
        parts[pl.ds(me_h, 1)] = part[...][None]
        for step in range(1, n_head):
            peer = (me_h + step) % n_head
            pltpu.make_async_remote_copy(
                src_ref=part, dst_ref=parts.at[peer], send_sem=send_p.at[peer],
                recv_sem=recv_p.at[peer], device_id={"head": peer}, device_id_type=MESH,
            ).wait_recv()
        total_part = parts[0]
        for slot in range(1, n_head):
            total_part = total_part + parts[slot]
        inv_row = lax.rsqrt(total_part[0:4] / features + EPSILON)
        pull_row = (inv_row * inv_row) * total_part[4:8] / features
        both = jnp.concatenate([inv_row, pull_row], axis=0)
        turned = jnp.concatenate([both] * (hd // 8), axis=0).T
        inv = jnp.broadcast_to(turned[:, 0:1], (rows, hd))
        pull = jnp.broadcast_to(turned[:, 4:5], (rows, hd))
        square_acc[...] = inv
        dot_acc[...] = pull

        @pl.loop(0, heads)
        def _(h):
            inv, pull = square_acc[...], dot_acc[...]
            att = attended[:, cols(h)]
            gain_h = gain[pl.ds(h, 1), :]
            grad_gain = g[:, cols(h)].astype(F32) * gain_h
            normed[:, cols(h)] = (att * inv * gain_h).astype(BF16)
            grad_h = (inv * (grad_gain - att * pull)).astype(BF16)
            grad_out[:, cols(h)] = grad_h
            fade = jnp.exp(entry_far[...] * decay_row(h))
            scaled = (q[:, cols(h)].astype(F32) * fade).astype(BF16)
            local2[pl.ds(h * owners, owners)] = matmul(scaled.T, grad_h).reshape(
                owners, rows_own, hd
            )

        spread(local2, inbox2, send3, recv3)
        inbox2[pl.ds(me, 1)] = local2[pl.ds(me, 1)]
        outs = [
            pltpu.make_async_copy(src, dst, out_sem.at[i])
            for i, (src, dst) in enumerate(
                ((normed, normed_hbm), (qg, qg_hbm), (kg, kg_hbm), (vg, vg_hbm))
            )
        ]
        outs[0].start()

        def backward(h):
            rate = decay_row(h)
            grad_h, key_h, value_h = grad_out[:, cols(h)], k[:, cols(h)], v[:, cols(h)]
            query_t, grad_t = q[:, cols(h)].T, grad_h.T
            high, low = halves(state1[pl.ds(h * owners, owners)].reshape(hd, hd))
            far = matmul_t(twice(grad_h), jnp.concatenate([high, low], axis=1))
            fade = jnp.exp(entry_far[...] * rate)
            far = far * fade
            key_sum = jnp.zeros((hd, rows), F32)
            value_sum = jnp.zeros((hd, rows), F32)
            for lo, hi in tiles:
                scores = matmul_t(grad_h[lo:hi], value_h[:hi])
                inner = jnp.exp(spacing[lo:hi, :hi] * wide(rate, hi))
                gw = (scores * inner).astype(BF16)
                qg[lo:hi, cols(h)] = (matmul(gw, key_h[:hi]) + far[lo:hi]).astype(BF16)
                key_add = matmul(query_t[:, lo:hi], gw)
                value_add = matmul(grad_t[:, lo:hi], weights[h, lo:hi, :hi])
                if hi < rows:
                    rest = jnp.zeros((hd, rows - hi), F32)
                    key_add = jnp.concatenate([key_add, rest], axis=1)
                    value_add = jnp.concatenate([value_add, rest], axis=1)
                key_sum = key_sum + key_add
                value_sum = value_sum + value_add
            key_part[:, cols(h)] = key_sum.T
            value_part[:, cols(h)] = value_sum.T

        @pl.loop(0, half)
        def _(h):
            backward(h)

        arrived_all(inbox2, recv3, send3)
        prefix(inbox2, outbox2, state2, True)
        spread(outbox2, state2, send4, recv4)

        @pl.loop(half, heads)
        def _(h):
            backward(h)

        outs[1].start()
        arrived_all(state2, recv4, send4)

        @pl.loop(0, heads)
        def _(h):
            high, low = halves(state2[pl.ds(h * owners, owners)].reshape(hd, hd))
            fade = jnp.exp(exit_far[...] * decay_row(h))
            key_far = matmul_t(twice(v[:, cols(h)]), jnp.concatenate([high, low], axis=1))
            value_far = matmul(twice(k[:, cols(h)]), jnp.concatenate([high, low], axis=0))
            kg[:, cols(h)] = (key_part[:, cols(h)] + fade * key_far).astype(BF16)
            vg[:, cols(h)] = (value_part[:, cols(h)] + fade * value_far).astype(BF16)

        outs[2].start()
        outs[3].start()
        left_all(local1, inbox1, send1, recv1)
        left_all(outbox1, state1, send2, recv2)
        left_all(local2, inbox2, send3, recv3)
        left_all(outbox2, state2, send4, recv4)
        for step in range(1, n_head):
            part_copy(step).wait_send()
        for out in outs:
            out.wait()

    return kernel


def solution(mesh):
    n_ctx, n_head = mesh.shape["ctx"], mesh.shape["head"]
    n_z = min(8, n_ctx)
    n_y = n_ctx // n_z

    def per_device(queries, keys, values, out_grad, gain, decay_rate, doc_lengths):
        rows, width = queries.shape
        heads = decay_rate.shape[0]
        hd = width // heads
        rows_own = heads * hd // n_ctx
        kernel = make_kernel(n_ctx, n_head, n_y, n_z, rows, heads, hd, width * n_head)
        wide16 = pltpu.VMEM((rows, width), BF16)
        wide32 = pltpu.VMEM((rows, width), F32)
        column = pltpu.VMEM((rows, hd), F32)
        slices = pltpu.VMEM((n_ctx, rows_own, hd), F32)
        dma = pltpu.SemaphoreType.DMA
        out = jax.ShapeDtypeStruct((rows, width), BF16)
        anywhere = pl.BlockSpec(memory_space=pl.ANY)
        scalars = pl.BlockSpec(memory_space=pltpu.SMEM)
        return pl.pallas_call(
            kernel,
            out_shape=(out,) * 4,
            in_specs=[scalars, scalars, pl.BlockSpec(memory_space=pltpu.VMEM)] + [anywhere] * 4,
            out_specs=(anywhere,) * 4,
            scratch_shapes=[wide16] * 8
            + [slices] * 8
            + [
                pltpu.VMEM((heads, rows, rows), BF16),
                wide32,
                wide16,
                pltpu.VMEM((rows, rows), F32),
                column,
                column,
                column,
                column,
                pltpu.VMEM((8, rows), F32),
                pltpu.VMEM((n_head, 8, rows), F32),
                wide32,
                wide32,
                pltpu.VMEM((n_ctx, hd), F32),
                dma((4,)),
                dma((4,)),
            ]
            + [dma((n_ctx,))] * 8
            + [dma((n_head,))] * 2,
            compiler_params=pltpu.CompilerParams(
                collective_id=0, has_side_effects=True, vmem_limit_bytes=56 * 2**20
            ),
        )(doc_lengths, decay_rate, gain.reshape(heads, hd), queries, keys, values, out_grad)

    in_specs = (P("ctx", "head"),) * 4 + (P("head"), P("head"), P())
    return jax.shard_map(
        per_device, mesh=mesh, in_specs=in_specs, out_specs=(P("ctx", "head"),) * 4, check_vma=False
    )
```

time: 419 us -> 90.7 us (0.22)
  waiting for transfers between devices: 182 us -> 0 us
  Pallas kernels: 0 us -> 83.3 us
  other arithmetic: 82.1 us -> 0 us
  blocking collectives: 77.9 us -> 0 us
  matrix products: 35.6 us -> 0 us
  between operations: 16.3 us -> 0.65 us
  local copies, waits for them, and re-layouts: 19.2 us -> 6.53 us
    all_gather x2 -> x0, waiting for transfers between devices: 182 us -> none  [prefix(): everything = jax.tree.map(lambda part: lax.all_gather(part, axis), value)]
    pallas_call x0 -> x1, Pallas kernels: none -> 83.3 us  [per_device(): pl.pallas_call(kernel, out_shape=(out,) * 4, in_specs=[scalars, scalars,...]
    select_n x65 -> x0, other arithmetic: 75.4 us -> none  [the longest x64 75.3 us: lap(): return jax.tree.map(lambda a, b: jnp.where(reached, a, b), new, before)]
    unnamed x1 -> x0, blocking collectives: 64.9 us -> none
    dot_general x12 -> x0, matrix products: 35.6 us -> none  [the longest x1 5.02 us: per_device(): jnp.einsum('thd,hde->the', query_wide, state_before, precision=FULL_PRECI...]
    psum x1 -> x0, blocking collectives: 13 us -> none  [per_device(): square_sum, dot_sum = lax.psum((square_part, dot_part), 'head')]
    unnamed x34 -> x10, local copies, waits for them, and re-layouts: 15.3 us -> 6.53 us
  transfers between devices with their start and end apart: 2 -> 0, of which waited for: 2 -> 0; matrix products, arithmetic and copies ran while one was open for 7% -> 0% of each run, Pallas kernels for 0% -> 0%
where the time goes in v1:
time: 90.7 us; the launch traced here: 90.5 us
  Pallas kernels  83.3 us (92%)
  local copies, waits for them, and re-layouts  6.53 us (7%)
    pallas_call x1, Pallas kernels, per_device(): pl.pallas_call(kernel, out_shape=(out,) * 4, in_specs=[scalars, scalars,...  83.3 us
    unnamed x10, local copies, waits for them, and re-layouts  6.53 us

profile of v1, /device:TPU:1, one launch (start us, length us, event | category | flops | bytes accessed | tf_op | source)
XLA Modules:
  0.0 90.5 jit_solution(7518707424109927569)
XLA Ops:
  0.6 83.3 %shard_map.102 = (bf16[512,1024]{1,0:T(8,128)(2,1)}, bf16[512,1024]{1,0:T(8,128)(2,1)}, bf16[512,1024]{1,0:T(8,128)(2,1)}, bf16[512,1024]{1,0:T(8,128)(2,1)}) custom-call(s32[8]{0:T(128)} %lengths.1, s32[8]{0:T(128)} %rates.1, f32[8,128]{1,0:T(8,128)} %bitcast.1, bf16[512,1024]{1,0:T(8,128)(2,1)} %q_hbm.1, bf16[512,1024]{1,0:T(8,128)(2,1)} %k_hbm.1, ...), custom_call_target="tpu_custom_call" | custom-call | tf_op jit(solution)/shard_map/pallas_call | solution.py:348
  83.9 0.0 copy-start.2
  83.9 2.4 %copy.15 = bf16[512,1024]{1,0:T(8,128)(2,1)} copy(bf16[512,1024]{1,0:T(8,128)(2,1)} %get-tuple-element.8) | data formatting | bytes 2097152
  86.3 0.0 copy-done.2
  86.3 0.0 copy-start.1
  86.3 1.0 %copy.16 = bf16[512,1024]{1,0:T(8,128)(2,1)} copy(bf16[512,1024]{1,0:T(8,128)(2,1)S(1)} %copy-done.2) | data formatting | bytes 2097152
  87.3 0.6 copy-done.1
  87.9 0.0 copy-start
  87.9 1.0 %copy.17 = bf16[512,1024]{1,0:T(8,128)(2,1)} copy(bf16[512,1024]{1,0:T(8,128)(2,1)S(1)} %copy-done.1) | data formatting | bytes 2097152
  88.9 0.6 copy-done
  89.5 1.0 %copy.18 = bf16[512,1024]{1,0:T(8,128)(2,1)} copy(bf16[512,1024]{1,0:T(8,128)(2,1)S(1)} %copy-done) | data formatting | bytes 2097152
Async XLA Ops:
  83.9 2.4 %copy-start.2 = (bf16[512,1024]{1,0:T(8,128)(2,1)S(1)}, bf16[512,1024]{1,0:T(8,128)(2,1)}, u32[]{:S(2)}) copy-start(bf16[512,1024]{1,0:T(8,128)(2,1)} %get-tuple-element.9) | copy-start | bytes 3145732
  86.3 1.6 %copy-start.1 = (bf16[512,1024]{1,0:T(8,128)(2,1)S(1)}, bf16[512,1024]{1,0:T(8,128)(2,1)}, u32[]{:S(2)}) copy-start(bf16[512,1024]{1,0:T(8,128)(2,1)} %get-tuple-element.10) | copy-start | bytes 3145732
  87.9 1.6 %copy-start = (bf16[512,1024]{1,0:T(8,128)(2,1)S(1)}, bf16[512,1024]{1,0:T(8,128)(2,1)}, u32[]{:S(2)}) copy-start(bf16[512,1024]{1,0:T(8,128)(2,1)} %get-tuple-element.11) | copy-start | bytes 3145732

commit v2 on v1

--- a/solution.py
+++ b/solution.py
@@ -8,6 +8,7 @@
 EPSILON = 1e-05
 FAR = 1e30
 TILE = 256
+UNROLL = 2
 MESH = pl.DeviceIdType.MESH
 F32, BF16 = jnp.float32, jnp.bfloat16
 
@@ -38,12 +39,12 @@
 
     def kernel(
         lengths, rates, gain, q_hbm, k_hbm, v_hbm, g_hbm,
-        normed_hbm, qg_hbm, kg_hbm, vg_hbm,
-        q, k, v, g, normed, qg, kg, vg,
+        normed, qg, kg, vg,
+        q, k, v, g,
         local1, inbox1, outbox1, state1, local2, inbox2, outbox2, state2,
         weights, attended, grad_out, spacing, entry_far, exit_far,
         square_acc, dot_acc, part, parts, key_part, value_part, carry_table,
-        in_sem, out_sem, send1, recv1, send2, recv2, send3, recv3, send4, recv4, send_p, recv_p,
+        in_sem, send1, recv1, send2, recv2, send3, recv3, send4, recv4, send_p, recv_p,
     ):
         me = lax.axis_index("ctx")
         me_h = lax.axis_index("head")
@@ -93,6 +94,10 @@
             return pl.ds(pl.multiple_of(h * hd, hd), hd)
 
         own_head = me // owners
+
+        def far_first(i):
+            return (own_head + heads // 2 + i) % heads
+
         block = lax.broadcasted_iota(jnp.int32, (n_ctx, hd), 0)
         inside = jnp.zeros((n_ctx, hd), jnp.int32)
         for end in ends:
@@ -119,6 +124,25 @@
                     src_ref=src.at[peer], dst_ref=dst.at[me], send_sem=send.at[peer],
                     recv_sem=recv.at[me], device_id={"ctx": peer}, device_id_type=MESH,
                 ).start()
+
+        def spread_head(h, src, dst, send, recv):
+            for piece in range(owners):
+                peer = h * owners + piece
+
+                @pl.when(peer != me)
+                def _():
+                    pltpu.make_async_remote_copy(
+                        src_ref=src.at[peer], dst_ref=dst.at[me], send_sem=send.at[peer],
+                        recv_sem=recv.at[me], device_id={"ctx": peer}, device_id_type=MESH,
+                    ).start()
+
+        def arrived_head(h, dst, recv, send):
+            for piece in range(owners):
+                peer = h * owners + piece
+
+                @pl.when(peer != me)
+                def _():
+                    arrived(dst, recv, send, peer)
 
         def arrived(dst, recv, send, slot):
             pltpu.make_async_remote_copy(
@@ -189,12 +213,13 @@
         def _(h):
             forward(h)
 
-        arrived_all(state1, recv2, send2)
         square_acc[...] = jnp.zeros_like(square_acc)
         dot_acc[...] = jnp.zeros_like(dot_acc)
 
-        @pl.loop(0, heads)
-        def _(h):
+        @pl.loop(0, heads, unroll=UNROLL)
+        def _(i):
+            h = far_first(i)
+            arrived_head(h, state1, recv2, send2)
             high, low = halves(state1[pl.ds(h * owners, owners)].reshape(hd, hd))
             far = matmul(twice(q[:, cols(h)]), jnp.concatenate([high, low], axis=0))
             fade = jnp.exp(entry_far[...] * decay_row(h))
@@ -237,8 +262,8 @@
         square_acc[...] = inv
         dot_acc[...] = pull
 
-        @pl.loop(0, heads)
-        def _(h):
+        def local_grad(i):
+            h = far_first(i)
             inv, pull = square_acc[...], dot_acc[...]
             att = attended[:, cols(h)]
             gain_h = gain[pl.ds(h, 1), :]
@@ -252,15 +277,15 @@
                 owners, rows_own, hd
             )
 
-        spread(local2, inbox2, send3, recv3)
+        local_grad(0)
+
+        @pl.loop(1, heads, unroll=True)
+        def _(i):
+            local_grad(i)
+            spread_head(far_first(i - 1), local2, inbox2, send3, recv3)
+
+        spread_head(far_first(heads - 1), local2, inbox2, send3, recv3)
         inbox2[pl.ds(me, 1)] = local2[pl.ds(me, 1)]
-        outs = [
-            pltpu.make_async_copy(src, dst, out_sem.at[i])
-            for i, (src, dst) in enumerate(
-                ((normed, normed_hbm), (qg, qg_hbm), (kg, kg_hbm), (vg, vg_hbm))
-            )
-        ]
-        outs[0].start()
 
         def backward(h):
             rate = decay_row(h)
@@ -300,11 +325,11 @@
         def _(h):
             backward(h)
 
-        outs[1].start()
-        arrived_all(state2, recv4, send4)
-
-        @pl.loop(0, heads)
-        def _(h):
+
+        @pl.loop(0, heads, unroll=UNROLL)
+        def _(i):
+            h = far_first(i)
+            arrived_head(h, state2, recv4, send4)
             high, low = halves(state2[pl.ds(h * owners, owners)].reshape(hd, hd))
             fade = jnp.exp(exit_far[...] * decay_row(h))
             key_far = matmul_t(twice(v[:, cols(h)]), jnp.concatenate([high, low], axis=1))
@@ -312,16 +337,12 @@
             kg[:, cols(h)] = (key_part[:, cols(h)] + fade * key_far).astype(BF16)
             vg[:, cols(h)] = (value_part[:, cols(h)] + fade * value_far).astype(BF16)
 
-        outs[2].start()
-        outs[3].start()
         left_all(local1, inbox1, send1, recv1)
         left_all(outbox1, state1, send2, recv2)
         left_all(local2, inbox2, send3, recv3)
         left_all(outbox2, state2, send4, recv4)
         for step in range(1, n_head):
             part_copy(step).wait_send()
-        for out in outs:
-            out.wait()
 
     return kernel
 
@@ -342,15 +363,14 @@
         column = pltpu.VMEM((rows, hd), F32)
         slices = pltpu.VMEM((n_ctx, rows_own, hd), F32)
         dma = pltpu.SemaphoreType.DMA
-        out = jax.ShapeDtypeStruct((rows, width), BF16)
         anywhere = pl.BlockSpec(memory_space=pl.ANY)
         scalars = pl.BlockSpec(memory_space=pltpu.SMEM)
         return pl.pallas_call(
             kernel,
-            out_shape=(out,) * 4,
+            out_shape=(wide16,) * 4,
             in_specs=[scalars, scalars, pl.BlockSpec(memory_space=pltpu.VMEM)] + [anywhere] * 4,
-            out_specs=(anywhere,) * 4,
-            scratch_shapes=[wide16] * 8
+            out_specs=(pl.BlockSpec(memory_space=pltpu.VMEM),) * 4,
+            scratch_shapes=[wide16] * 4
             + [slices] * 8
             + [
                 pltpu.VMEM((heads, rows, rows), BF16),
@@ -367,7 +387,6 @@
                 wide32,
                 pltpu.VMEM((n_ctx, hd), F32),
                 dma((4,)),
-                dma((4,)),
             ]
             + [dma((n_ctx,))] * 8
             + [dma((n_head,))] * 2,

time: 90.7 us -> 83.7 us (0.923)
  Pallas kernels: 83.3 us -> 79 us
  local copies, waits for them, and re-layouts: 6.53 us -> 3.88 us
    pallas_call x1, Pallas kernels: 83.3 us -> 79 us  [per_device(): pl.pallas_call(kernel, out_shape=(wide16,) * 4, in_specs=[scalars, scalar...]
    unnamed x10 -> x4, local copies, waits for them, and re-layouts: 6.53 us -> 3.88 us
where the time goes in v2:
time: 83.7 us; the launch traced here: 83.5 us
  Pallas kernels  79 us (94%)
  local copies, waits for them, and re-layouts  3.88 us (5%)
    pallas_call x1, Pallas kernels, per_device(): pl.pallas_call(kernel, out_shape=(wide16,) * 4, in_specs=[scalars, scalar...  79 us
    unnamed x4, local copies, waits for them, and re-layouts  3.88 us

profile of v2, /device:TPU:1, one launch (start us, length us, event | category | flops | bytes accessed | tf_op | source)
XLA Modules:
  0.0 83.5 jit_solution(14729702452864365296)
XLA Ops:
  0.6 79.0 %shard_map.102 = (bf16[512,1024]{1,0:T(8,128)(2,1)S(1)}, bf16[512,1024]{1,0:T(8,128)(2,1)S(1)}, bf16[512,1024]{1,0:T(8,128)(2,1)S(1)}, bf16[512,1024]{1,0:T(8,128)(2,1)S(1)}) custom-call(s32[8]{0:T(128)} %lengths.1, s32[8]{0:T(128)} %rates.1, f32[8,128]{1,0:T(8,128)} %bitcast.1, bf16[512,1024]{1,0:T(8,128)(2,1)} %q_hbm.1, bf16[512,1024]{1,0:T(8,128)(2,1)} %k_hbm.1, ...), custom_call_target="tpu_custom_call" | custom-call | tf_op jit(solution)/shard_map/pallas_call | solution.py:368
  79.7 1.0 %copy.15 = bf16[512,1024]{1,0:T(8,128)(2,1)} copy(bf16[512,1024]{1,0:T(8,128)(2,1)S(1)} %get-tuple-element.4) | data formatting | bytes 2097152
  80.6 1.0 %copy.16 = bf16[512,1024]{1,0:T(8,128)(2,1)} copy(bf16[512,1024]{1,0:T(8,128)(2,1)S(1)} %get-tuple-element.5) | data formatting | bytes 2097152
  81.6 1.0 %copy.17 = bf16[512,1024]{1,0:T(8,128)(2,1)} copy(bf16[512,1024]{1,0:T(8,128)(2,1)S(1)} %get-tuple-element.6) | data formatting | bytes 2097152
  82.6 1.0 %copy.18 = bf16[512,1024]{1,0:T(8,128)(2,1)} copy(bf16[512,1024]{1,0:T(8,128)(2,1)S(1)} %get-tuple-element.7) | data formatting | bytes 2097152

commit v3 on v2

--- a/solution.py
+++ b/solution.py
@@ -8,7 +8,7 @@
 EPSILON = 1e-05
 FAR = 1e30
 TILE = 256
-UNROLL = 2
+UNROLL = 4
 MESH = pl.DeviceIdType.MESH
 F32, BF16 = jnp.float32, jnp.bfloat16
 
@@ -43,7 +43,7 @@
         q, k, v, g,
         local1, inbox1, outbox1, state1, local2, inbox2, outbox2, state2,
         weights, attended, grad_out, spacing, entry_far, exit_far,
-        square_acc, dot_acc, part, parts, key_part, value_part, carry_table,
+        square_acc, dot_acc, part, parts, key_part, value_part, carry_table, query_scaled,
         in_sem, send1, recv1, send2, recv2, send3, recv3, send4, recv4, send_p, recv_p,
     ):
         me = lax.axis_index("ctx")
@@ -182,6 +182,8 @@
         def forward(h):
             rate = decay_row(h)
             key_h, value_h = k[:, cols(h)], v[:, cols(h)]
+            fade = jnp.exp(entry_far[...] * rate)
+            query_scaled[h] = (q[:, cols(h)].astype(F32) * fade).astype(BF16).T
             for lo, hi in tiles:
                 scores = matmul_t(q[lo:hi, cols(h)], key_h[:hi])
                 inner = jnp.exp(spacing[lo:hi, :hi] * wide(rate, hi))
@@ -203,7 +205,7 @@
                 outbox[pl.ds(j, 1)] = carried[None]
                 return carried * carry_table[pl.ds(j, 1), :] + inbox[j]
 
-            lax.fori_loop(0, n_ctx, lap, jnp.zeros((rows_own, hd), F32))
+            lax.fori_loop(0, n_ctx, lap, jnp.zeros((rows_own, hd), F32), unroll=4)
             state[pl.ds(me, 1)] = outbox[pl.ds(me, 1)]
 
         prefix(inbox1, outbox1, state1, False)
@@ -268,12 +270,9 @@
             att = attended[:, cols(h)]
             gain_h = gain[pl.ds(h, 1), :]
             grad_gain = g[:, cols(h)].astype(F32) * gain_h
-            normed[:, cols(h)] = (att * inv * gain_h).astype(BF16)
             grad_h = (inv * (grad_gain - att * pull)).astype(BF16)
             grad_out[:, cols(h)] = grad_h
-            fade = jnp.exp(entry_far[...] * decay_row(h))
-            scaled = (q[:, cols(h)].astype(F32) * fade).astype(BF16)
-            local2[pl.ds(h * owners, owners)] = matmul(scaled.T, grad_h).reshape(
+            local2[pl.ds(h * owners, owners)] = matmul(query_scaled[h], grad_h).reshape(
                 owners, rows_own, hd
             )
 
@@ -289,6 +288,8 @@
 
         def backward(h):
             rate = decay_row(h)
+            gain_h = gain[pl.ds(h, 1), :]
+            normed[:, cols(h)] = (attended[:, cols(h)] * square_acc[...] * gain_h).astype(BF16)
             grad_h, key_h, value_h = grad_out[:, cols(h)], k[:, cols(h)], v[:, cols(h)]
             query_t, grad_t = q[:, cols(h)].T, grad_h.T
             high, low = halves(state1[pl.ds(h * owners, owners)].reshape(hd, hd))
@@ -386,6 +387,7 @@
                 wide32,
                 wide32,
                 pltpu.VMEM((n_ctx, hd), F32),
+                pltpu.VMEM((heads, hd, rows), BF16),
                 dma((4,)),
             ]
             + [dma((n_ctx,))] * 8

time: 83.7 us -> 83.3 us (level)
  no operation moved by 1% of the time
where the time goes in v3:
time: 83.3 us; the launch traced here: 83.2 us
  Pallas kernels  78.7 us (94%)
  local copies, waits for them, and re-layouts  3.88 us (5%)
    pallas_call x1, Pallas kernels, per_device(): pl.pallas_call(kernel, out_shape=(wide16,) * 4, in_specs=[scalars, scalar...  78.7 us
    unnamed x4, local copies, waits for them, and re-layouts  3.88 us

profile of v3, /device:TPU:1, one launch (start us, length us, event | category | flops | bytes accessed | tf_op | source)
XLA Modules:
  0.0 83.2 jit_solution(18308166435440313446)
XLA Ops:
  0.6 78.7 %shard_map.102 = (bf16[512,1024]{1,0:T(8,128)(2,1)S(1)}, bf16[512,1024]{1,0:T(8,128)(2,1)S(1)}, bf16[512,1024]{1,0:T(8,128)(2,1)S(1)}, bf16[512,1024]{1,0:T(8,128)(2,1)S(1)}) custom-call(s32[8]{0:T(128)} %lengths.1, s32[8]{0:T(128)} %rates.1, f32[8,128]{1,0:T(8,128)} %bitcast.1, bf16[512,1024]{1,0:T(8,128)(2,1)} %q_hbm.1, bf16[512,1024]{1,0:T(8,128)(2,1)} %k_hbm.1, ...), custom_call_target="tpu_custom_call" | custom-call | tf_op jit(solution)/shard_map/pallas_call | solution.py:369
  79.3 1.0 %copy.15 = bf16[512,1024]{1,0:T(8,128)(2,1)} copy(bf16[512,1024]{1,0:T(8,128)(2,1)S(1)} %get-tuple-element.4) | data formatting | bytes 2097152
  80.3 1.0 %copy.16 = bf16[512,1024]{1,0:T(8,128)(2,1)} copy(bf16[512,1024]{1,0:T(8,128)(2,1)S(1)} %get-tuple-element.5) | data formatting | bytes 2097152
  81.3 1.0 %copy.17 = bf16[512,1024]{1,0:T(8,128)(2,1)} copy(bf16[512,1024]{1,0:T(8,128)(2,1)S(1)} %get-tuple-element.6) | data formatting | bytes 2097152
  82.3 1.0 %copy.18 = bf16[512,1024]{1,0:T(8,128)(2,1)} copy(bf16[512,1024]{1,0:T(8,128)(2,1)S(1)} %get-tuple-element.7) | data formatting | bytes 2097152

commit v4 on v3

--- a/solution.py
+++ b/solution.py
@@ -8,7 +8,7 @@
 EPSILON = 1e-05
 FAR = 1e30
 TILE = 256
-UNROLL = 4
+UNROLL = 8
 MESH = pl.DeviceIdType.MESH
 F32, BF16 = jnp.float32, jnp.bfloat16
 

time: 83.3 us -> 83.4 us (level)
  no operation moved by 1% of the time
where the time goes in v4:
time: 83.4 us; the launch traced here: 83.3 us
  Pallas kernels  78.8 us (94%)
  local copies, waits for them, and re-layouts  3.88 us (5%)
    pallas_call x1, Pallas kernels, per_device(): pl.pallas_call(kernel, out_shape=(wide16,) * 4, in_specs=[scalars, scalar...  78.8 us
    unnamed x4, local copies, waits for them, and re-layouts  3.88 us

profile of v4, /device:TPU:1, one launch (start us, length us, event | category | flops | bytes accessed | tf_op | source)
XLA Modules:
  0.0 83.3 jit_solution(4003795270042658594)
XLA Ops:
  0.6 78.8 %shard_map.102 = (bf16[512,1024]{1,0:T(8,128)(2,1)S(1)}, bf16[512,1024]{1,0:T(8,128)(2,1)S(1)}, bf16[512,1024]{1,0:T(8,128)(2,1)S(1)}, bf16[512,1024]{1,0:T(8,128)(2,1)S(1)}) custom-call(s32[8]{0:T(128)} %lengths.1, s32[8]{0:T(128)} %rates.1, f32[8,128]{1,0:T(8,128)} %bitcast.1, bf16[512,1024]{1,0:T(8,128)(2,1)} %q_hbm.1, bf16[512,1024]{1,0:T(8,128)(2,1)} %k_hbm.1, ...), custom_call_target="tpu_custom_call" | custom-call | tf_op jit(solution)/shard_map/pallas_call | solution.py:369
  79.4 1.0 %copy.15 = bf16[512,1024]{1,0:T(8,128)(2,1)} copy(bf16[512,1024]{1,0:T(8,128)(2,1)S(1)} %get-tuple-element.4) | data formatting | bytes 2097152
  80.4 1.0 %copy.16 = bf16[512,1024]{1,0:T(8,128)(2,1)} copy(bf16[512,1024]{1,0:T(8,128)(2,1)S(1)} %get-tuple-element.5) | data formatting | bytes 2097152
  81.4 1.0 %copy.17 = bf16[512,1024]{1,0:T(8,128)(2,1)} copy(bf16[512,1024]{1,0:T(8,128)(2,1)S(1)} %get-tuple-element.6) | data formatting | bytes 2097152
  82.3 1.0 %copy.18 = bf16[512,1024]{1,0:T(8,128)(2,1)} copy(bf16[512,1024]{1,0:T(8,128)(2,1)S(1)} %get-tuple-element.7) | data formatting | bytes 2097152
